TPU v7x, 128 devices: a whole 4x4x4 slice. The times are simulated.
128 devices in a mesh: req: 2 (over core), ctx: 64 (over y, z, x).
Axes of the slice: x: 4, y: 4, z: 4, core: 2. Of those that a mesh axis runs over, the one named last changes fastest.
Arguments:
- queries: bfloat16 [128, 8192], P(('req', 'ctx')), parts along dimension 0, may hold values from -256 to 256
- new_kv: bfloat16 [128, 2, 1024], P(('req', 'ctx')), parts along dimension 0, may hold values from -12 to 12
- prefix_kv: bfloat16 [8, 65536, 2, 1024], P('req', 'ctx'), parts along dimension 0, may hold values from -4.5 to 4.5
- pool: bfloat16 [1024, 16, 2, 1024], P(('req', 'ctx')), parts along dimension 0, may hold values from -12 to 12
- out_weight: bfloat16 [8192, 8192], P('ctx'), may hold values from -0.0625 to 0.0625
- parents: int32 [128], P('req'), parts along dimension 0, may hold values from 0 to 63, as said below
- tail_table: int32 [128, 4], P('req'), parts along dimension 0, may hold values from 0 to 511, as said below
- fresh_slots: int32 [128], P('req'), parts along dimension 0, may hold values from 0 to 511, as said below
- tail_lengths: int32 [128], P('req'), parts along dimension 0, may hold values from 1 to 63
Outputs:
- attn_out: float32 [128, 8192], P(('req', 'ctx')), parts along dimension 0
- new_pool: bfloat16 [1024, 16, 2, 1024], P(('req', 'ctx')), parts along dimension 0
There are 2 independent parts, one for each index of `req`. A program takes and returns all parts, laid end to end along the dimension named above; an argument that names none is the same for every part. Nothing has to cross between parts.
Inputs may be any that keep to these rules, and one draw needn't show every extreme that they name: `parents`: row i's parent is a beam of the same request, from 16 * (i // 16) to that plus 16 - 1. `tail_table`: all entries are distinct pool blocks, none among the last 2 blocks of a device's 8. Distinct pool blocks; fresh_slots[i] is one of the last 2 blocks of the device that holds beam row i, that is of device i.
All inputs are finite; a program needn't handle non-finite values.
Results may differ from a plain program's by a relative error of at most 0.0055.
Values may be sent and summed in bfloat16 or wider, within the bound.
A program may use at most 384 MiB of HBM per device.

v0:
```python
import jax
import jax.numpy as jnp
from jax import lax
from jax.sharding import PartitionSpec as P

HQ = 64
KVH = 8
HD = 128
CAP = 2


masked_score = -1e30


def joined(array, axis, combine):
    everything = jax.tree.map(lambda part: lax.all_gather(part, axis), array)
    initial = jax.tree.map(lambda part: part[0], everything)

    def step(k, so_far):
        return combine(so_far, jax.tree.map(lambda part: part[k], everything))

    return lax.fori_loop(1, lax.axis_size(axis), step, initial)


def combine_parts(former, latter):
    highest = jnp.maximum(former[0], latter[0])
    former_weight = jnp.exp(former[0] - highest)
    latter_weight = jnp.exp(latter[0] - highest)
    totals = former[1] * former_weight + latter[1] * latter_weight
    output = former[2] * former_weight[..., None] + latter[2] * latter_weight[..., None]
    return (highest, totals, output)


def narrow(values):
    return values.astype(jnp.bfloat16)


def local(
    queries, new_kv, prefix_kv, pool, out_weight, parents, tail_table, fresh_slots, tail_lengths
):
    devices = lax.axis_size("ctx")
    my_index = lax.axis_index("ctx")
    local_rows = queries.shape[0]
    row_total = local_rows * devices
    pool_dev = pool.shape[0]
    block_len = pool.shape[1]
    kv_width = pool.shape[3]
    requests = prefix_kv.shape[0]
    local_len = prefix_kv.shape[1]
    table_depth = tail_table.shape[1]
    capacity = CAP
    groups = HQ // KVH
    beam_count = row_total // requests
    scaling = HD ** (-0.5)
    flat_width = block_len * 2 * kv_width
    parent_len = tail_lengths[parents]
    parent_table = tail_table[parents]
    offset = parent_len % block_len
    source = jnp.take_along_axis(parent_table, (parent_len // block_len)[:, None], axis=1)[:, 0]
    target_dev = fresh_slots // pool_dev
    target_pos = fresh_slots % pool_dev - (pool_dev - capacity)
    position = jnp.arange(block_len, dtype=jnp.int32)
    row_ids = jnp.arange(row_total, dtype=jnp.int32)
    owns_source = source // pool_dev == my_index
    owns_row = row_ids // local_rows == my_index
    picked = pool[jnp.clip(source - my_index * pool_dev, 0, pool_dev - 1)]
    keep_old = owns_source[:, None] & (position[None, :] < offset[:, None])
    kept = jnp.where(keep_old[:, :, None, None], picked, jnp.zeros((), jnp.bfloat16))
    slot_range = jnp.arange(capacity, dtype=jnp.int32)
    bucket = target_dev * capacity + target_pos
    write_new = owns_row[:, None] & (position[None, :] == offset[:, None])
    token_full = lax.dynamic_update_slice_in_dim(
        jnp.zeros((row_total, 2, kv_width), jnp.bfloat16), new_kv, my_index * local_rows, 0
    )
    contrib = jnp.where(write_new[:, :, None, None], token_full[:, None], kept)
    outgoing = jnp.zeros((devices * capacity, flat_width), jnp.bfloat16)
    outgoing = outgoing.at[bucket].set(contrib.reshape(row_total, flat_width))
    filled = jnp.any(
        (target_dev[:, None] == my_index) & (target_pos[:, None] == slot_range[None, :]), axis=0
    )
    incoming = lax.all_to_all(outgoing, "ctx", split_axis=0, concat_axis=0, tiled=True)
    arrived = jnp.sum(incoming.reshape(devices, capacity, flat_width), axis=0, dtype=jnp.float32)
    arrived = arrived.astype(jnp.bfloat16).reshape(capacity, block_len, 2, kv_width)
    previous = pool[pool_dev - capacity :]
    new_pool = jnp.concatenate(
        [pool[: pool_dev - capacity], jnp.where(filled[:, None, None, None], arrived, previous)],
        axis=0,
    )
    everyone = lax.all_gather(queries, "ctx", axis=0, tiled=True)
    query_grid = everyone.reshape(requests, beam_count, KVH, groups, HD)
    pre_keys = prefix_kv[:, :, 0].reshape(requests, local_len, KVH, HD)
    pre_vals = prefix_kv[:, :, 1].reshape(requests, local_len, KVH, HD)
    pre_score = (
        jnp.einsum("rbkgd,rpkd->kgrbp", query_grid, pre_keys, preferred_element_type=jnp.float32)
        * scaling
    )
    pre_score = pre_score.reshape(KVH, groups, row_total, local_len)
    flat_query = everyone.reshape(row_total, KVH, groups, HD)
    pool_keys = pool[:, :, 0].reshape(pool_dev * block_len, KVH, HD)
    pool_vals = pool[:, :, 1].reshape(pool_dev * block_len, KVH, HD)
    tail_score = (
        jnp.einsum("ikgd,tkd->kgit", flat_query, pool_keys, preferred_element_type=jnp.float32)
        * scaling
    )
    slot_ids = my_index * pool_dev + jnp.arange(pool_dev, dtype=jnp.int32)
    matches = parent_table[:, :, None] == slot_ids[None, None, :]
    reach_limit = (
        parent_len[:, None] - jnp.arange(table_depth, dtype=jnp.int32)[None, :] * block_len
    )
    live_mask = jnp.any(
        matches[:, :, :, None] & (position[None, None, None, :] < reach_limit[:, :, None, None]),
        axis=1,
    )
    live_mask = live_mask.reshape(row_total, pool_dev * block_len)
    tail_score = jnp.where(live_mask[None, None], tail_score, masked_score)
    own_query = queries.reshape(local_rows, KVH, groups, HD)
    own_keys = new_kv[:, 0].reshape(local_rows, KVH, HD)
    own_score = (
        jnp.einsum("ikgd,ikd->kgi", own_query, own_keys, preferred_element_type=jnp.float32)
        * scaling
    )
    new_score = lax.dynamic_update_slice_in_dim(
        jnp.full((KVH, groups, row_total), masked_score, jnp.float32),
        own_score,
        my_index * local_rows,
        2,
    )
    value_full = lax.dynamic_update_slice_in_dim(
        jnp.zeros((row_total, kv_width), jnp.bfloat16), new_kv[:, 1], my_index * local_rows, 0
    )
    new_vals = value_full.reshape(row_total, KVH, HD)
    highest = jnp.maximum(jnp.maximum(pre_score.max(-1), tail_score.max(-1)), new_score)
    pre_exp = jnp.exp(pre_score - highest[..., None])
    tail_exp = jnp.exp(tail_score - highest[..., None])
    new_exp = jnp.exp(new_score - highest)
    totals = pre_exp.sum(-1) + tail_exp.sum(-1) + new_exp
    pre_weights = narrow(pre_exp).reshape(KVH, groups, requests, beam_count, local_len)
    pre_out = jnp.einsum(
        "kgrbp,rpkd->kgrbd", pre_weights, pre_vals, preferred_element_type=jnp.float32
    )
    part_out = pre_out.reshape(KVH, groups, row_total, HD)
    part_out = part_out + jnp.einsum(
        "kgit,tkd->kgid", narrow(tail_exp), pool_vals, preferred_element_type=jnp.float32
    )
    part_out = part_out + jnp.einsum(
        "kgi,ikd->kgid", narrow(new_exp), new_vals, preferred_element_type=jnp.float32
    )
    part_max = highest.reshape(HQ, row_total)
    part_sum = totals.reshape(HQ, row_total)
    part_out = part_out.reshape(HQ, row_total, HD)
    own_heads = HQ // devices
    merged = joined((part_max, part_sum, part_out), "ctx", combine_parts)
    head_sum = lax.dynamic_slice_in_dim(merged[1], my_index * own_heads, own_heads, 0)
    head_out = lax.dynamic_slice_in_dim(merged[2], my_index * own_heads, own_heads, 0)
    attended = (head_out / head_sum[..., None]).astype(jnp.bfloat16)
    flat_heads = attended.transpose(1, 0, 2).reshape(row_total, own_heads * HD)
    result = lax.psum_scatter(
        jnp.dot(flat_heads, out_weight, preferred_element_type=jnp.float32),
        "ctx",
        scatter_dimension=0,
        tiled=True,
    )
    return (result, new_pool)


def solution(mesh):
    in_specs = (
        P(("req", "ctx"), None),
        P(("req", "ctx"), None, None),
        P("req", "ctx", None, None),
        P(("req", "ctx"), None, None, None),
        P("ctx", None),
        P("req"),
        P("req", None),
        P("req"),
        P("req"),
    )
    out_specs = (P(("req", "ctx"), None), P(("req", "ctx"), None, None, None))
    return jax.shard_map(local, mesh=mesh, in_specs=in_specs, out_specs=out_specs, check_vma=False)
```

profile of v0, /device:TPU:0, one launch (start us, length us, event | category | flops | bytes accessed | tf_op | source)
XLA Modules:
  0.0 1286.7 jit_solution(2451278584269422486)
XLA Ops:
  8.8 32.3 %fusion.44 = (bf16[4,1024,1,1024]{3,2,1,0:T(2,128)(2,1)}, bf16[4,1024,1,1024]{3,2,1,0:T(2,128)(2,1)}) fusion(bf16[4,1024,2,1024]{3,2,1,0:T(2,128)(2,1)} %param.13), kind=kLoop, calls=%fused_computation.119 | loop fusion | bytes 33554432 | tf_op jit(solution)/shard_map/slice | solution.py:92
  41.4 38.9 %copy.107 = bf16[4,1024,1,1024]{1,3,0,2:T(8,128)(2,1)} copy(bf16[4,1024,1,1024]{3,2,1,0:T(2,128)(2,1)} %get-tuple-element.208) | data formatting | bytes 16777216
  84.9 8.9 reduce.4
  96.2 12.1 bitcast_reduce_fusion
  112.9 38.8 %copy.108 = bf16[4,1024,1,1024]{1,3,0,2:T(8,128)(2,1)} copy(bf16[4,1024,1,1024]{3,2,1,0:T(2,128)(2,1)} %get-tuple-element.207) | data formatting | bytes 16777216
  152.5 7.8 fusion.5
  163.8 10.2 fusion.17
  179.0 10.4 gather_fusion.2
  189.7 7.5 broadcast_select_fusion.1
  197.2 7.8 reshape.428
  204.9 12.4 scatter_custom_fusion
  217.3 14.1 %all_to_all.6 = bf16[64,2,32768]{2,1,0:T(2,128)(2,1)} reshape(bf16[128,32768]{1,0:T(8,128)(2,1)} %scatter_custom_fusion) | data formatting | bytes 16777216 | tf_op jit(solution)/shard_map/all_to_all | solution.py:81
  231.4 12.4 all-to-all-start
  244.6 22.5 %all-gather.8.cloned.1.call-done = f32[64,64,64]{2,1,0:T(8,128)} async-done(((f32[1,64,64]{2,1,0:T(8,128)}), f32[64,64,64]{2,1,0:T(8,128)}) %all-gather.8.cloned.1.call-update) | async-done | bytes 1048592 | tf_op jit(solution)/shard_map/all_gather | solution.py:16
  267.9 580.3 %all-gather.10.cloned.1.call-done = f32[64,64,64,128]{3,2,1,0:T(8,128)} async-done(((f32[1,64,64,128]{3,2,1,0:T(8,128)}), f32[64,64,64,128]{3,2,1,0:T(8,128)}) %all-gather.10.cloned.1.call-update) | async-done | bytes 134217744 | tf_op jit(solution)/shard_map/all_gather | solution.py:16
  851.3 291.4 %while.19 = (s32[]{:T(128)}, f32[64,64]{1,0:T(8,128)S(1)}, f32[64,64]{1,0:T(8,128)S(1)}, f32[64,64,128]{2,1,0:T(8,128)}, f32[64,64,64]{2,1,0:T(8,128)}, /*index=...) while((s32[]{:T(128)}, f32[64,64]{1,0:T(8,128)S(1)}, ...), condition=%wide.region_6.7_spmd, body=%wide.region_5.6_spmd.sunk | while | flops 1597445 | bytes 6455447 | solution.py:22
  880.1 3.8 fusion.50
  884.7 3.8 fusion.50
  889.3 3.8 fusion.50
  893.9 3.8 fusion.50
  898.6 3.8 fusion.50
  903.2 3.8 fusion.50
  967.9 3.8 fusion.50
  972.5 3.8 fusion.50
  977.1 3.8 fusion.50
  981.8 3.8 fusion.50
  986.4 3.8 fusion.50
  991.0 3.8 fusion.50
  1055.7 3.8 fusion.50
  1060.3 3.8 fusion.50
  1146.2 8.3 reduce_sum.35
  1156.3 121.4 %all-reduce.3.cloned.1.call-done = f32[64,8192]{1,0:T(8,128)} async-done(((f32[64,8192]{1,0:T(8,128)}), f32[64,8192]{1,0:T(8,128)}) %all-reduce.3.cloned.1.call-update) | async-done | bytes 2097168
  (213 shorter events, 272.9 us)
Async XLA Ops:
  7.2 1135.5 %copy-start = (bf16[128,8192]{1,0:T(8,128)(2,1)S(1)}, bf16[128,8192]{1,0:T(8,128)(2,1)}, u32[]{:S(2)}) copy-start(bf16[128,8192]{1,0:T(8,128)(2,1)} %param.15) | copy-start | bytes 6291460
  7.2 77.7 %all-gather.12.cloned.1.call-start = ((), (), s32[]{:S(2)}) async-start(), calls=%async_computation.4 | async-start | bytes 2129920 | tf_op jit(solution)/shard_map/all_gather | solution.py:89
  7.9 236.0 %all-gather.6.cloned.1.call-start = ((), (), s32[]{:S(2)}) async-start(), calls=%async_computation.1 | async-start | bytes 2129920 | tf_op jit(solution)/shard_map/all_gather | solution.py:16
  8.8 32.3 %copy-start.5 = (bf16[1,2,1024]{2,1,0:T(2,128)(2,1)S(1)}, bf16[1,2,1024]{2,1,0:T(2,128)(2,1)}, u32[]{:S(2)}) copy-start(bf16[1,2,1024]{2,1,0:T(2,128)(2,1)} %param.12) | copy-start | bytes 12292
  41.4 38.9 %copy-start.2 = (bf16[8,16,2,1024]{3,2,1,0:T(2,128)(2,1)S(1)}, bf16[8,16,2,1024]{3,2,1,0:T(2,128)(2,1)}, u32[]{:S(2)}) copy-start(bf16[8,16,2,1024]{3,2,1,0:T(2,128)(2,1)} %param.14) | copy-start | bytes 1572868
  41.4 41.1 %copy-start.6 = (s32[64,4]{0,1:T(4,128)S(1)}, s32[64,4]{0,1:T(4,128)}, u32[]{:S(2)}) copy-start(s32[64,4]{0,1:T(4,128)} %param.17) | copy-start | bytes 3076
  41.4 41.2 %copy-start.7 = (s32[64]{0:T(128)S(1)}, s32[64]{0:T(128)}, u32[]{:S(2)}) copy-start(s32[64]{0:T(128)} %param.18) | copy-start | bytes 772
  41.4 41.2 %copy-start.8 = (s32[64]{0:T(128)S(1)}, s32[64]{0:T(128)}, u32[]{:S(2)}) copy-start(s32[64]{0:T(128)} %param.16) | copy-start | bytes 772
  41.4 41.3 %copy-start.1 = (s32[64]{0:T(128)S(1)}, s32[64]{0:T(128)}, u32[]{:S(2)}) copy-start(s32[64]{0:T(128)} %param.19) | copy-start | bytes 772
  112.8 154.3 %all-gather.8.cloned.1.call-start = ((), (), s32[]{:S(2)}) async-start(), calls=%async_computation.2 | async-start | bytes 2129920 | tf_op jit(solution)/shard_map/all_gather | solution.py:16
  112.9 39.4 %copy-start.4 = (f32[8,8,64]{2,1,0:T(8,128)S(1)}, f32[8,8,64]{2,1,0:T(8,128)}, u32[]{:S(2)}) copy-start(f32[8,8,64]{2,1,0:T(8,128)} %get-tuple-element.206) | copy-start | bytes 49156
  163.6 684.6 %all-gather.10.cloned.1.call-start = ((), (), s32[]{:S(2)}) async-start(), calls=%async_computation.3 | async-start | bytes 136314880 | tf_op jit(solution)/shard_map/all_gather | solution.py:16
  174.0 1.6 copy-start.3
  231.4 914.8 %all-to-all-start = ((bf16[64,2,32768]{2,1,0:T(2,128)(2,1)}), bf16[64,2,32768]{2,1,0:T(2,128)(2,1)}, u32[]{:S(2)}, u32[]{:S(2)}) async-start(bf16[64,2,32768]{2,1,0:T(2,128)(2,1)} %all_to_all.6), calls=%async_computation | async-start | bytes 16777216 | tf_op jit(solution)/shard_map/all_to_all | solution.py:81
  243.8 1033.9 %all-reduce.3.cloned.1.call-start = ((), (), s32[]{:S(2)}) async-start(), calls=%async_computation.5 | async-start | bytes 4194304
  1142.7 2.6 copy-start.9
  1146.1 8.7 slice-start
Sparse Core Ops, SparseCore 0:
  10.9 68.1 all-gather.11
  112.9 68.7 all-gather.5
  185.2 81.8 all-gather.7
  269.9 578.2 all-gather.9
  1145.5 132.1 all-reduce.2
where the time goes:
time: 1300 us; the launch traced here: 1290 us
  waiting for transfers between devices  725 us (56%)
  other arithmetic  330 us (25%)
  local copies, waits for them, and re-layouts  173 us (13%)
  matrix products  31.1 us (2%)
  between operations  14.4 us (1%)
    all_gather x3, waiting for transfers between devices, joined(): everything = jax.tree.map(lambda part: lax.all_gather(part, axis), array)  603 us
    add x63, other arithmetic, combine_parts(): former[2] * former_weight[..., None] + latter[2] * latter_weight[..., None]  240 us
    unnamed x6, waiting for transfers between devices  122 us
    unnamed x30, local copies, waits for them, and re-layouts  84.7 us
    add x63, other arithmetic, combine_parts(): totals = former[1] * former_weight + latter[1] * latter_weight  51 us
    slice x1, local copies, waits for them, and re-layouts, local(): pre_vals = prefix_kv[:, :, 1].reshape(requests, local_len, KVH, HD)  32.3 us
  transfers between devices with their start and end apart: 6, of which 3 were waited for; matrix products, arithmetic and copies ran while one was open for 38% of the time, Pallas kernels for 0%

commit v1 on v0

v1 whole, which is shorter than its diff:
```python
import functools
import math

import jax
import jax.numpy as jnp
from jax import lax
from jax.experimental import pallas as pl
from jax.experimental.pallas import tpu as pltpu
from jax.sharding import PartitionSpec as P

KVH = 8
HD = 128
GROUPS = 8
HQ = 64
N = 64
REQS = 4
BEAMS = 16
PRE = 1024
CHUNK = 128
PER_REQ = PRE // CHUNK
CHUNKS = REQS * PER_REQ
SLOTS = 4
TOKROWS = 16
BLK = 8
OLD = 6
NEG = -1e30
SCALE = HD ** (-0.5) * math.log2(math.e)
MESH = pl.DeviceIdType.MESH
F32 = jnp.float32
BF16 = jnp.bfloat16
PARTS = ((0, 3, "xzy"), (3, 6, "zyx"), (6, 8, "yxz"))


def dot_nt(a, b):
    return lax.dot_general(a, b, (((1,), (1,)), ((), ())), preferred_element_type=F32)


def dot_nn(a, b):
    return jnp.dot(a, b, preferred_element_type=F32)


def kernel(
    parents, table, fresh, lens, q_ref, newkv_ref, kv_hbm, pool_hbm, w_hbm,
    out_ref, newpool_ref,
    raw, stg, kd, kt, poolv, qstg, qbuf, qd, bias, osend, orecv, stat, srecv,
    wv, ystg, ysend, yrecv, relay, p2send, p2recv, blk,
    kv_sem, misc_sem, out_sem, q_ssem, q_rsem, o_ssem, o_rsem, s_ssem, s_rsem,
    y_ssem, y_rsem, p_ssem, p_rsem,
):
    core = lax.axis_index("req")
    me = lax.axis_index("ctx")
    y, z, x = me // 16, me // 4 % 4, me % 4

    def at(dy, dz, dx):
        return ((y + dy) % 4 * 4 + (z + dz) % 4) * 4 + (x + dx) % 4

    def peer(k):
        return at(k // 16, k // 4 % 4, k % 4)

    def remote(src, dst, ssem, rsem, dev):
        return pltpu.make_async_remote_copy(
            src_ref=src, dst_ref=dst, send_sem=ssem, recv_sem=rsem,
            device_id=(core, dev), device_id_type=MESH,
        )

    def await_bytes(ref, sem):
        pltpu.make_async_copy(ref, ref, sem).wait()

    def kv_copy(c):
        return pltpu.make_async_copy(
            kv_hbm.at[c // PER_REQ, pl.ds(c % PER_REQ * (CHUNK * TOKROWS), CHUNK * TOKROWS)],
            raw.at[c % SLOTS], kv_sem.at[c % SLOTS],
        )

    pool_copy = pltpu.make_async_copy(pool_hbm, poolv, misc_sem.at[0])
    w_copy = pltpu.make_async_copy(w_hbm, wv, misc_sem.at[1])
    pool_copy.start()
    for c in range(SLOTS):
        kv_copy(c).start()

    barrier = pltpu.get_barrier_semaphore()

    def greet(k, _):
        pl.semaphore_signal(barrier, inc=1, device_id=(core, peer(k)), device_id_type=MESH)
        return 0

    lax.fori_loop(1, N, greet, 0)

    for h in range(HQ):
        qstg[h : h + 1, :] = q_ref[:, h * HD : (h + 1) * HD].astype(F32)
    qbuf[y, z, x] = qstg[0:HQ, :].astype(BF16).reshape(KVH, GROUPS, HD)
    pl.semaphore_wait(barrier, N - 1)

    def q_copies(phase):
        made = []
        for p, (g0, g1, order) in enumerate(PARTS):
            axis = order[phase]
            seen = order[:phase]
            index = (
                slice(None) if "y" in seen else y,
                slice(None) if "z" in seen else z,
                slice(None) if "x" in seen else x,
                slice(g0, g1),
            )
            for d in range(1, 4):
                dev = at(d * (axis == "y"), d * (axis == "z"), d * (axis == "x"))
                made.append(remote(
                    qbuf.at[index], qbuf.at[index],
                    q_ssem.at[phase * 3 + p], q_rsem.at[phase * 3 + p], dev,
                ))
        return made

    def q_region(phase, p):
        g0, g1, _ = PARTS[p]
        rows = (
            (0, slice(0, 1), slice(0, 3)),
            (0, slice(0, 3), slice(None)),
            (slice(0, 3), slice(None), slice(None)),
        )[phase]
        return qbuf.at[rows + (slice(g0, g1),)]

    def q_send(phase):
        for copy in q_copies(phase):
            copy.start()

    def q_wait(phase):
        for p in range(3):
            await_bytes(q_region(phase, p), q_rsem.at[phase * 3 + p])

    q_send(0)

    pool_copy.wait()
    w_copy.start()

    def spread(dst, base):
        for j in range(TOKROWS):
            dst[j // 2, j % 2, pl.ds(base, CHUNK), :] = stg[
                pl.ds(j, CHUNK, stride=TOKROWS), :
            ].astype(BF16)

    stg[...] = poolv[...].reshape(CHUNK * TOKROWS, HD).astype(F32)
    stg[OLD * 16 * TOKROWS : (OLD * 16 + 1) * TOKROWS, :] = newkv_ref[...].astype(F32)
    spread(kt, 0)

    def piece(j):
        return poolv.at[pl.ds(j // 32 * 3, 3), j % 32]

    def to_relay(k, _):
        j = peer(k)
        remote(piece(j), relay.at[me], p_ssem.at[0], p_rsem.at[0], j).start()
        return 0

    lax.fori_loop(1, N, to_relay, 0)
    relay[me] = poolv[pl.ds(me // 32 * 3, 3), me % 32]

    lane = lax.broadcasted_iota(jnp.int32, (1, 128), 1)

    def mask_row(i, _):
        par = parents[i]
        length = lens[par]
        live = (lane == OLD * 16) & (jnp.full((1, 128), i, jnp.int32) == me)
        for j in range(4):
            block = table[j, par] - me * BLK
            live = live | ((lane // 16 == block) & (lane % 16 < length - 16 * j))
        bias[pl.ds(i, 1), :] = jnp.where(live, 0.0, NEG)
        return 0

    lax.fori_loop(0, N, mask_row, 0)

    def chunks(lo, hi):
        def body(c, _):
            kv_copy(c).wait()
            stg[...] = raw[c % SLOTS].astype(F32)

            @pl.when(c + SLOTS < CHUNKS)
            def _():
                kv_copy(c + SLOTS).start()

            spread(kd.at[c // PER_REQ], pl.multiple_of(c % PER_REQ * CHUNK, CHUNK))
            return 0

        lax.fori_loop(lo, hi, body, 0)

    chunks(0, 8)
    q_wait(0)
    q_send(1)
    chunks(8, 16)
    q_wait(1)
    q_send(2)
    chunks(16, 32)
    q_wait(2)

    await_bytes(relay.at[0:63], p_rsem.at[0])
    first = me // 32 * 3

    def pick(i, _):
        par = parents[i]
        source = table[lens[par] // 16, par]
        held = jnp.clip(source % BLK - first, 0, 2)
        p2send[i] = relay[source // BLK, held]
        return 0

    lax.fori_loop(0, N, pick, 0)

    def to_row(k, _):
        j = peer(k)
        remote(p2send.at[j], p2recv.at[me], p_ssem.at[1], p_rsem.at[1], j).start()
        return 0

    lax.fori_loop(1, N, to_row, 0)
    p2recv[me] = p2send[me]

    stat[...] = jnp.zeros_like(stat)
    sub16 = lax.broadcasted_iota(jnp.int32, (BEAMS, 128), 0)
    lane16 = lax.broadcasted_iota(jnp.int32, (BEAMS, 128), 1)

    def request(r, _):
        qstg[...] = qbuf[r].reshape(BEAMS * HQ, HD).astype(F32)
        for h in range(HQ):
            qd[h // GROUPS, h % GROUPS * BEAMS : (h % GROUPS + 1) * BEAMS, :] = qstg[
                pl.ds(h, BEAMS, stride=HQ), :
            ].astype(BF16)
        bias_r = bias[pl.ds(pl.multiple_of(r * BEAMS, BEAMS), BEAMS), :]
        bias_q = jnp.broadcast_to(bias_r[None], (GROUPS, BEAMS, 128)).reshape(128, 128)
        m_spot = lane16 == sub16 + r * BEAMS
        l_spot = lane16 == sub16 + r * BEAMS + 64

        def head(g, _):
            q = qd[g]
            s = dot_nt(q, kd[r, g, 0])
            st = dot_nt(q, kt[g, 0]) + bias_q
            top = jnp.maximum(s.max(-1, keepdims=True), st.max(-1, keepdims=True))
            e = jnp.exp2((s - top) * SCALE)
            et = jnp.exp2((st - top) * SCALE)
            total = e.sum(-1, keepdims=True) + et.sum(-1, keepdims=True)
            o = dot_nn(e.astype(BF16), kd[r, g, 1]) + dot_nn(et.astype(BF16), kt[g, 1])
            osend[r, pl.ds(g * GROUPS, GROUPS)] = o.astype(BF16).reshape(GROUPS, BEAMS, HD)
            top3 = jnp.broadcast_to(top, (128, 128)).reshape(GROUPS, BEAMS, 128)
            total3 = jnp.broadcast_to(total, (128, 128)).reshape(GROUPS, BEAMS, 128)
            both = jnp.where(m_spot[None], top3, jnp.where(l_spot[None], total3, 0.0))
            rows = pl.ds(pl.multiple_of(g * GROUPS, GROUPS), GROUPS)
            stat[rows, :] = stat[rows, :] + both.sum(1)
            return 0

        lax.fori_loop(0, KVH, head, 0)

        def send(k, _):
            j = peer(k)
            remote(osend.at[r, j], orecv.at[me, r], o_ssem.at[r], o_rsem.at[r], j).start()
            return 0

        lax.fori_loop(1, N, send, 0)
        orecv[me, r] = osend[r, me]
        return 0

    lax.fori_loop(0, REQS, request, 0)

    def send_stat(k, _):
        j = peer(k)
        remote(stat.at[pl.ds(j, 1)], srecv.at[pl.ds(me, 1)], s_ssem, s_rsem, j).start()
        return 0

    lax.fori_loop(1, N, send_stat, 0)
    srecv[pl.ds(me, 1), :] = stat[pl.ds(me, 1), :]

    await_bytes(p2recv.at[0:63], p_rsem.at[1])
    par = parents[me]
    length = lens[par]
    source = table[length // 16, par]
    half = source % BLK // 3 * 32
    off = length % 16
    kept_all = p2recv[pl.ds(half, 32)].astype(F32)
    stg[0 : 32 * 8, :] = kept_all.reshape(32 * 8, HD)
    slot = fresh[me] % BLK
    newkv = newkv_ref[...].astype(F32)
    for t in range(16):
        rows = slice(t * TOKROWS, (t + 1) * TOKROWS)
        where_t = jnp.full((TOKROWS, HD), t, jnp.int32)
        token = jnp.where(where_t < off, stg[rows, :], jnp.where(where_t == off, newkv, 0.0))
        for b in range(2):
            here = jnp.full((TOKROWS, HD), OLD + b, jnp.int32) == slot
            old = poolv[OLD + b, 2 * t : 2 * t + 2].astype(F32).reshape(TOKROWS, HD)
            blk[b, 2 * t : 2 * t + 2] = jnp.where(here, token, old).astype(BF16).reshape(2, 8, HD)
    keep_copy = pltpu.make_async_copy(poolv.at[0:OLD], newpool_ref.at[0:OLD], out_sem.at[0])
    new_copy = pltpu.make_async_copy(blk, newpool_ref.at[OLD:BLK], out_sem.at[1])
    keep_copy.start()
    new_copy.start()

    await_bytes(srecv.at[0:63], s_rsem)
    turned = srecv[...].T
    valid = lax.broadcasted_iota(jnp.int32, (64, 128), 1) < N
    tops = jnp.where(valid, turned[0:64], -3e38)
    sums = jnp.where(valid, turned[64:128], 0.0)
    top = tops.max(-1, keepdims=True)
    share = jnp.exp2((tops - top) * SCALE)
    share = share / (share * sums).sum(-1, keepdims=True)
    for r in range(REQS):
        await_bytes(orecv.at[0:63, r], o_rsem.at[r])
    acc = jnp.zeros((64, HD), F32)
    for s in range(N):
        acc = acc + share[:, s : s + 1] * orecv[s].reshape(64, HD).astype(F32)
    attended = acc.astype(BF16)

    w_copy.wait()
    for c in range(16):
        part = dot_nn(attended, wv[:, c * 512 : (c + 1) * 512])
        for j in range(4):
            ystg[pl.ds(c * 4 + j, N, stride=64), :] = part[:, j * HD : (j + 1) * HD]

    def pack(i, _):
        ysend[i] = ystg[pl.ds(pl.multiple_of(i * 64, 64), 64), :].astype(BF16)
        return 0

    lax.fori_loop(0, N, pack, 0)

    def send_y(k, _):
        j = peer(k)
        remote(ysend.at[j], yrecv.at[me], y_ssem, y_rsem, j).start()
        return 0

    lax.fori_loop(1, N, send_y, 0)
    yrecv[me] = ysend[me]
    await_bytes(yrecv.at[0:63], y_rsem)

    def add(s, total):
        return total + yrecv[s].astype(F32)

    out_ref[...] = lax.fori_loop(0, N, add, jnp.zeros((64, HD), F32))

    for phase in range(3):
        for p in range(3):
            await_bytes(q_region(phase, p), q_ssem.at[phase * 3 + p])
    await_bytes(relay.at[0:63], p_ssem.at[0])
    await_bytes(p2send.at[0:63], p_ssem.at[1])
    for r in range(REQS):
        await_bytes(orecv.at[0:63, r], o_ssem.at[r])
    await_bytes(srecv.at[0:63], s_ssem)
    await_bytes(ysend.at[0:63], y_ssem)
    keep_copy.wait()
    new_copy.wait()


def local(
    queries, new_kv, prefix_kv, pool, out_weight, parents, tail_table, fresh_slots, tail_lengths
):
    def rows_of(a):
        lead = a.shape[:-2]
        a = a.reshape(lead + (2, KVH, HD))
        k = len(lead)
        return a.transpose(tuple(range(k)) + (k + 1, k, k + 2))

    kv = rows_of(prefix_kv).reshape(REQS, PRE * TOKROWS, HD)
    pool_rows = rows_of(pool).reshape(BLK, 32, 8, HD)
    new_rows = rows_of(new_kv).reshape(TOKROWS, HD)
    smem = pl.BlockSpec(memory_space=pltpu.SMEM)
    vmem = pl.BlockSpec(memory_space=pltpu.VMEM)
    hbm = pl.BlockSpec(memory_space=pl.ANY)
    dma = pltpu.SemaphoreType.DMA
    out, new_pool = pl.pallas_call(
        kernel,
        out_shape=(
            jax.ShapeDtypeStruct((64, HD), F32),
            jax.ShapeDtypeStruct((BLK, 32, 8, HD), BF16),
        ),
        in_specs=[smem] * 4 + [vmem, vmem, hbm, hbm, hbm],
        out_specs=(vmem, hbm),
        scratch_shapes=[
            pltpu.VMEM((SLOTS, CHUNK * TOKROWS, HD), BF16),
            pltpu.VMEM((CHUNK * TOKROWS, HD), F32),
            pltpu.VMEM((REQS, KVH, 2, PRE, HD), BF16),
            pltpu.VMEM((KVH, 2, CHUNK, HD), BF16),
            pltpu.VMEM((BLK, 32, 8, HD), BF16),
            pltpu.VMEM((BEAMS * HQ, HD), F32),
            pltpu.VMEM((4, 4, 4, KVH, GROUPS, HD), BF16),
            pltpu.VMEM((KVH, 128, HD), BF16),
            pltpu.VMEM((N, 128), F32),
            pltpu.VMEM((REQS, HQ, BEAMS, HD), BF16),
            pltpu.VMEM((N, REQS, BEAMS, HD), BF16),
            pltpu.VMEM((HQ, 128), F32),
            pltpu.VMEM((128, 128), F32),
            pltpu.VMEM((HD, 8192), BF16),
            pltpu.VMEM((N * 64, HD), F32),
            pltpu.VMEM((N, 64, HD), BF16),
            pltpu.VMEM((N, 64, HD), BF16),
            pltpu.VMEM((N, 3, 8, HD), BF16),
            pltpu.VMEM((N, 8, HD), BF16),
            pltpu.VMEM((N, 8, HD), BF16),
            pltpu.VMEM((2, 32, 8, HD), BF16),
            dma((SLOTS,)), dma((2,)), dma((2,)),
            dma((9,)), dma((9,)), dma((REQS,)), dma((REQS,)), dma, dma,
            dma, dma, dma((2,)), dma((2,)),
        ],
        compiler_params=pltpu.CompilerParams(
            collective_id=0, has_side_effects=True, vmem_limit_bytes=56 << 20
        ),
        name="beam_decode",
    )(
        parents, tail_table.T, fresh_slots, tail_lengths,
        queries, new_rows, kv, pool_rows, out_weight,
    )
    new_pool = new_pool.reshape(BLK, 16, KVH, 2, HD).transpose(0, 1, 3, 2, 4)
    return out.reshape(1, 8192), new_pool.reshape(BLK, 16, 2, KVH * HD)


def solution(mesh):
    in_specs = (
        P(("req", "ctx"), None),
        P(("req", "ctx"), None, None),
        P("req", "ctx", None, None),
        P(("req", "ctx"), None, None, None),
        P("ctx", None),
        P("req"),
        P("req", None),
        P("req"),
        P("req"),
    )
    out_specs = (P(("req", "ctx"), None), P(("req", "ctx"), None, None, None))
    return jax.shard_map(local, mesh=mesh, in_specs=in_specs, out_specs=out_specs, check_vma=False)
```

time: 1300 us -> 88.9 us (0.07)
  waiting for transfers between devices: 725 us -> 0 us
  other arithmetic: 330 us -> 0 us
  local copies, waits for them, and re-layouts: 173 us -> 3.57 us
  Pallas kernels: 0 us -> 84.4 us
  matrix products: 31.1 us -> 0 us
  between operations: 14.4 us -> 0.64 us
    all_gather x4 -> x0, waiting for transfers between devices: 603 us -> none  [the longest x3 603 us: joined(): everything = jax.tree.map(lambda part: lax.all_gather(part, axis), array)]
    add x127 -> x0, other arithmetic: 291 us -> none  [the longest x63 240 us: combine_parts(): former[2] * former_weight[..., None] + latter[2] * latter_weight[..., None]]
    unnamed x6 -> x0, waiting for transfers between devices: 122 us -> none
    pallas_call x0 -> x1, Pallas kernels: none -> 84.4 us  [local(): pl.pallas_call(kernel, out_shape=(jax.ShapeDtypeStruct((64, HD), F32), ja...]
    unnamed x30 -> x2, local copies, waits for them, and re-layouts: 84.7 us -> 3.57 us
    slice x4 -> x0, local copies, waits for them, and re-layouts: 34.4 us -> none  [the longest x1 32.3 us: local(): pre_vals = prefix_kv[:, :, 1].reshape(requests, local_len, KVH, HD)]
    dot_general x6 -> x0, matrix products: 31.1 us -> none  [the longest x1 12.1 us: local(): jnp.einsum('rbkgd,rpkd->kgrbp', query_grid, pre_keys, preferred_element_t...]
    reduce_sum x3 -> x0, other arithmetic: 18.6 us -> none  [the longest x2 10.3 us: local(): totals = pre_exp.sum(-1) + tail_exp.sum(-1) + new_exp]
  transfers between devices with their start and end apart: 6 -> 0, of which waited for: 3 -> 0; matrix products, arithmetic and copies ran while one was open for 38% -> 0% of each run, Pallas kernels for 0% -> 0%
where the time goes in v1:
time: 88.9 us; the launch traced here: 88.6 us
  Pallas kernels  84.4 us (95%)
  local copies, waits for them, and re-layouts  3.57 us (4%)
    pallas_call x1, Pallas kernels, local(): pl.pallas_call(kernel, out_shape=(jax.ShapeDtypeStruct((64, HD), F32), ja...  84.4 us
    unnamed x2, local copies, waits for them, and re-layouts  3.57 us

profile of v1, /device:TPU:0, one launch (start us, length us, event | category | flops | bytes accessed | tf_op | source)
XLA Modules:
  0.0 88.6 jit_solution(2920102368846296180)
XLA Ops:
  0.6 84.4 %beam_decode.1 = (f32[64,128]{1,0:T(8,128)}, bf16[8,32,8,128]{3,2,1,0:T(8,128)(2,1)}) custom-call(s32[64]{0:T(128)} %parents.1, s32[4,64]{1,0:T(4,128)} %bitcast.27, s32[64]{0:T(128)} %fresh.1, s32[64]{0:T(128)} %lens.1, bf16[1,8192]{1,0:T(2,128)(2,1)} %q_ref.1, bf16[16,128]{1,0:T(8,128)(2,1)} %bitcast.26, bf16[4,16384,128]{2,1,0:T(8,128)(2,1)} %bitcast.22, ...), custom_call_target="tpu_custom_call" | custom-call | tf_op jit(solution)/shard_map/beam_decode/pallas_call | solution.py:359
  85.0 1.4 %copy.17 = f32[1,8192]{1,0:T(1,128)} copy(f32[1,8192]{1,0:T(1,128)} %bitcast.25) | data formatting | bytes 65536
  86.4 2.2 %copy.18 = bf16[8,16,2,1024]{3,2,1,0:T(2,128)(2,1)} copy(bf16[8,16,2,1024]{3,2,1,0:T(2,128)(2,1)} %bitcast.24) | data formatting | bytes 1048576

commit v2 on v1

v2 whole, which is shorter than its diff:
```python
import functools
import math

import jax
import jax.numpy as jnp
from jax import lax
from jax.experimental import pallas as pl
from jax.experimental.pallas import tpu as pltpu
from jax.sharding import PartitionSpec as P

KVH = 8
HD = 128
GROUPS = 8
HQ = 64
N = 64
REQS = 4
BEAMS = 16
PRE = 1024
CHUNK = 128
PER_REQ = PRE // CHUNK
CHUNKS = REQS * PER_REQ
TOKROWS = 16
BLK = 8
OLD = 6
NEG = -1e30
SCALE = HD ** (-0.5) * math.log2(math.e)
MESH = pl.DeviceIdType.MESH
F32 = jnp.float32
BF16 = jnp.bfloat16
PARTS = ((0, 3, "xzy"), (3, 6, "zyx"), (6, 8, "yxz"))


def dot_nt(a, b):
    return lax.dot_general(a, b, (((1,), (1,)), ((), ())), preferred_element_type=F32)


def dot_nn(a, b):
    return jnp.dot(a, b, preferred_element_type=F32)


def kernel(
    parents, table, fresh, lens, q_ref, newkv_ref, kv_hbm, pool_hbm, w_hbm,
    out_ref, newpool_ref,
    raw, stg, kd, kt, poolv, poolz, qstg, qbuf, qd, bias, osend, orecv, stat, srecv,
    wv, ystg, ysend, y1, y2send, y2, y3send, y3, rx, rz, ry, p2send, p2x, p2z, p2y, blk,
    kv_sem, misc_sem, out_sem, q_ssem, q_rsem, o_ssem, o_rsem, s_ssem, s_rsem,
    y_ssem, y_rsem, p_ssem, p_rsem,
):
    core = lax.axis_index("req")
    me = lax.axis_index("ctx")
    y, z, x = me // 16, me // 4 % 4, me % 4

    def at(dy, dz, dx):
        return ((y + dy) % 4 * 4 + (z + dz) % 4) * 4 + (x + dx) % 4

    def remote(src, dst, ssem, rsem, dev):
        return pltpu.make_async_remote_copy(
            src_ref=src, dst_ref=dst, send_sem=ssem, recv_sem=rsem,
            device_id=(core, dev), device_id_type=MESH,
        )

    def await_bytes(ref, sem):
        pltpu.make_async_copy(ref, ref, sem).wait()

    def kv_copy(c):
        return pltpu.make_async_copy(
            kv_hbm.at[c // PER_REQ, pl.ds(c % PER_REQ * (CHUNK * TOKROWS), CHUNK * TOKROWS)],
            raw.at[c], kv_sem.at[c],
        )

    barrier = pltpu.get_barrier_semaphore()
    for d in range(1, 4):
        for dev in (at(d, 0, 0), at(0, d, 0), at(0, 0, d)):
            pl.semaphore_signal(barrier, inc=1, device_id=(core, dev), device_id_type=MESH)

    pool_copies = [
        pltpu.make_async_copy(pool_hbm.at[0:3], poolv.at[0], misc_sem.at[0]),
        pltpu.make_async_copy(pool_hbm.at[3:6], poolv.at[1], misc_sem.at[1]),
        pltpu.make_async_copy(pool_hbm.at[6:8], poolz, misc_sem.at[2]),
    ]
    w_copy = pltpu.make_async_copy(w_hbm, wv, misc_sem.at[3])
    for copy in pool_copies:
        copy.start()
    for c in range(CHUNKS):
        kv_copy(c).start()
    w_copy.start()

    for h in range(HQ):
        qstg[h : h + 1, :] = q_ref[:, h * HD : (h + 1) * HD].astype(F32)
    qbuf[y, z, x] = qstg[0:HQ, :].astype(BF16).reshape(KVH, GROUPS, HD)

    def q_copies(phase):
        made = []
        for p, (g0, g1, order) in enumerate(PARTS):
            axis = order[phase]
            seen = order[:phase]
            index = (
                slice(None) if "y" in seen else y,
                slice(None) if "z" in seen else z,
                slice(None) if "x" in seen else x,
                slice(g0, g1),
            )
            for d in range(1, 4):
                dev = at(d * (axis == "y"), d * (axis == "z"), d * (axis == "x"))
                made.append(remote(
                    qbuf.at[index], qbuf.at[index],
                    q_ssem.at[phase * 3 + p], q_rsem.at[phase * 3 + p], dev,
                ))
        return made

    def q_region(phase, p):
        g0, g1, _ = PARTS[p]
        rows = (
            (0, slice(0, 1), slice(0, 3)),
            (0, slice(0, 3), slice(None)),
            (slice(0, 3), slice(None), slice(None)),
        )[phase]
        return qbuf.at[rows + (slice(g0, g1),)]

    def q_send(phase):
        for copy in q_copies(phase):
            copy.start()

    def q_wait(phase):
        for p in range(3):
            await_bytes(q_region(phase, p), q_rsem.at[phase * 3 + p])

    for copy in pool_copies:
        copy.wait()

    def spread(dst, base):
        for j in range(TOKROWS):
            dst[j // 2, j % 2, pl.ds(base, CHUNK), :] = stg[
                pl.ds(j, CHUNK, stride=TOKROWS), :
            ].astype(BF16)

    stg[0 : OLD * 256, :] = poolv[...].reshape(OLD * 256, HD).astype(F32)
    stg[OLD * 256 :, :] = poolz[...].reshape((BLK - OLD) * 256, HD).astype(F32)
    stg[OLD * 256 : OLD * 256 + TOKROWS, :] = newkv_ref[...].astype(F32)
    spread(kt, 0)

    def along(d):
        return (y + d) % 4, (z + d) % 4, (x + d) % 4

    def leg1(phase):
        for d in range(1, 4):
            y2_, z2_, x2_ = along(d)
            src, dst, dev = (
                (poolv.at[:, :, :, :, x2_], rx.at[x], at(0, 0, d)),
                (rx.at[:, :, :, :, z2_], rz.at[z], at(0, d, 0)),
                (rz.at[:, :, y2_ // 2, :, y2_ % 2], ry.at[y], at(d, 0, 0)),
            )[phase]
            remote(src, dst, p_ssem.at[phase], p_rsem.at[phase], dev).start()
        if phase == 0:
            rx[x] = poolv[:, :, :, :, x]
        elif phase == 1:
            rz[z] = rx[:, :, :, :, z]
        else:
            ry[y] = rz[:, :, y // 2, :, y % 2]

    def leg1_wait(phase):
        await_bytes((rx, rz, ry)[phase].at[0:3], p_rsem.at[phase])

    def leg2(phase):
        for d in range(1, 4):
            y2_, z2_, x2_ = along(d)
            src, dst, dev = (
                (p2send.at[:, :, x2_], p2x.at[x], at(0, 0, d)),
                (p2x.at[:, :, z2_], p2z.at[z], at(0, d, 0)),
                (p2z.at[:, :, y2_], p2y.at[y], at(d, 0, 0)),
            )[phase]
            remote(src, dst, p_ssem.at[3 + phase], p_rsem.at[3 + phase], dev).start()
        if phase == 0:
            p2x[x] = p2send[:, :, x]
        elif phase == 1:
            p2z[z] = p2x[:, :, z]
        else:
            p2y[y] = p2z[:, :, y]

    def leg2_wait(phase):
        await_bytes((p2x, p2z, p2y)[phase].at[0:3], p_rsem.at[3 + phase])

    pl.semaphore_wait(barrier, 9)
    q_send(0)
    leg1(0)

    lane = lax.broadcasted_iota(jnp.int32, (1, 128), 1)

    def mask_row(i, _):
        par = parents[i]
        length = lens[par]
        live = (lane == OLD * 16) & (jnp.full((1, 128), i, jnp.int32) == me)
        for j in range(4):
            block = table[j, par] - me * BLK
            live = live | ((lane // 16 == block) & (lane % 16 < length - 16 * j))
        bias[pl.ds(i, 1), :] = jnp.where(live, 0.0, NEG)
        return 0

    lax.fori_loop(0, N, mask_row, 0, unroll=8)

    def chunks(lo, hi):
        def body(c, _):
            kv_copy(c).wait()
            stg[...] = raw[c].astype(F32)
            spread(kd.at[c // PER_REQ], pl.multiple_of(c % PER_REQ * CHUNK, CHUNK))
            return 0

        lax.fori_loop(lo, hi, body, 0)

    q_wait(0)
    q_send(1)
    chunks(0, 8)
    q_wait(1)
    q_send(2)
    leg1_wait(0)
    leg1(1)
    chunks(8, 32)
    q_wait(2)
    leg1_wait(1)
    leg1(2)

    first = me // 32 * 3

    def pick(i, _):
        par = parents[i]
        source = table[lens[par] // 16, par]
        held = jnp.clip(source % BLK - first, 0, 2)
        home = source // BLK
        p2send[i // 16, i // 4 % 4, i % 4] = ry[home // 16, home // 4 % 4, home % 4, held]
        return 0

    stat[...] = jnp.zeros_like(stat)
    sub16 = lax.broadcasted_iota(jnp.int32, (BEAMS, 128), 0)
    lane16 = lax.broadcasted_iota(jnp.int32, (BEAMS, 128), 1)

    def turn(r, _):
        qstg[...] = qbuf[r].reshape(BEAMS * HQ, HD).astype(F32)
        for h in range(HQ):
            qd[r, h // GROUPS, h % GROUPS * BEAMS : (h % GROUPS + 1) * BEAMS, :] = qstg[
                pl.ds(h, BEAMS, stride=HQ), :
            ].astype(BF16)
        return 0

    lax.fori_loop(0, REQS, turn, 0)
    own_group = me // GROUPS

    def group_of(t):
        return (own_group + t) % KVH

    def attend(t):
        r = t // KVH
        g = group_of(t)
        bias_r = bias[pl.ds(pl.multiple_of(r * BEAMS, BEAMS), BEAMS), :]
        bias_q = jnp.broadcast_to(bias_r[None], (GROUPS, BEAMS, 128)).reshape(128, 128)
        m_spot = lane16 == sub16 + r * BEAMS
        l_spot = lane16 == sub16 + r * BEAMS + 64
        q = qd[r, g]
        s = dot_nt(q, kd[r, g, 0])
        st = dot_nt(q, kt[g, 0]) + bias_q
        top = jnp.maximum(s.max(-1, keepdims=True), st.max(-1, keepdims=True))
        e = jnp.exp2((s - top) * SCALE)
        et = jnp.exp2((st - top) * SCALE)
        total = e.sum(-1, keepdims=True) + et.sum(-1, keepdims=True)
        o = dot_nn(e.astype(BF16), kd[r, g, 1]) + dot_nn(et.astype(BF16), kt[g, 1])
        osend[r, pl.ds(g * GROUPS, GROUPS)] = o.astype(BF16).reshape(GROUPS, BEAMS, HD)
        top3 = jnp.broadcast_to(top, (128, 128)).reshape(GROUPS, BEAMS, 128)
        total3 = jnp.broadcast_to(total, (128, 128)).reshape(GROUPS, BEAMS, 128)
        both = jnp.where(m_spot[None], top3, jnp.where(l_spot[None], total3, 0.0))
        rows = pl.ds(pl.multiple_of(g * GROUPS, GROUPS), GROUPS)
        stat[rows, :] = stat[rows, :] + both.sum(1)

    def send(t, last):
        r = t // KVH
        g = group_of(t)
        for j in range(GROUPS):
            dev = g * GROUPS + (me + j) % GROUPS

            def start(dev=dev):
                remote(osend.at[r, dev], orecv.at[me, r], o_ssem.at[r], o_rsem.at[r], dev).start()
                if last:
                    remote(
                        stat.at[pl.ds(dev, 1)], srecv.at[pl.ds(me, 1)], s_ssem, s_rsem, dev
                    ).start()

            if j == 0:
                pl.when(t % KVH != 0)(start)
            else:
                start()

    def steps(lo, hi, last):
        def step(t, _):
            send(t - 1, last)
            attend(t)
            return 0

        lax.fori_loop(lo, hi, step, 0)

    attend(0)
    steps(1, 8, False)
    leg1_wait(2)
    lax.fori_loop(0, N, pick, 0, unroll=8)
    leg2(0)
    steps(8, 16, False)
    leg2_wait(0)
    leg2(1)
    steps(16, 25, False)
    leg2_wait(1)
    leg2(2)
    steps(25, 32, True)
    send(jnp.int32(31), True)
    for r in range(REQS):
        orecv[me, r] = osend[r, me]
    srecv[pl.ds(me, 1), :] = stat[pl.ds(me, 1), :]

    leg2_wait(2)
    par = parents[me]
    length = lens[par]
    source = table[length // 16, par]
    half = source % BLK // 3 * 2
    off = length % 16
    kept_all = p2y[pl.ds(half, 2)].astype(F32)
    stg[0 : 32 * 8, :] = kept_all.reshape(32 * 8, HD)
    slot = fresh[me] % BLK
    newkv = newkv_ref[...].astype(F32)
    for t in range(16):
        rows = slice(t * TOKROWS, (t + 1) * TOKROWS)
        where_t = jnp.full((TOKROWS, HD), t, jnp.int32)
        token = jnp.where(where_t < off, stg[rows, :], jnp.where(where_t == off, newkv, 0.0))
        for b in range(2):
            here = jnp.full((TOKROWS, HD), OLD + b, jnp.int32) == slot
            at_t = (b, t // 8, t // 2 % 4, slice(t % 2 * 2, t % 2 * 2 + 2))
            old = poolz[at_t].astype(F32).reshape(TOKROWS, HD)
            blk[at_t] = jnp.where(here, token, old).astype(BF16).reshape(2, 8, HD)
    keep_copies = [
        pltpu.make_async_copy(poolv.at[0], newpool_ref.at[0:3], out_sem.at[0]),
        pltpu.make_async_copy(poolv.at[1], newpool_ref.at[3:6], out_sem.at[1]),
        pltpu.make_async_copy(blk, newpool_ref.at[6:8], out_sem.at[2]),
    ]
    for copy in keep_copies:
        copy.start()

    await_bytes(srecv.at[0:63], s_rsem)
    turned = srecv[...].T
    valid = lax.broadcasted_iota(jnp.int32, (64, 128), 1) < N
    tops = jnp.where(valid, turned[0:64], -3e38)
    sums = jnp.where(valid, turned[64:128], 0.0)
    top = tops.max(-1, keepdims=True)
    share = jnp.exp2((tops - top) * SCALE)
    share = share / (share * sums).sum(-1, keepdims=True)
    for r in range(REQS):
        await_bytes(orecv.at[0:63, r], o_rsem.at[r])
    acc = jnp.zeros((64, HD), F32)
    for s in range(N):
        acc = acc + share[:, s : s + 1] * orecv[s].reshape(64, HD).astype(F32)
    attended = acc.astype(BF16)

    w_copy.wait()

    def y_pick(ref, order, phase, index, c0, c1):
        rows = []
        for name in "yzx":
            if name in order[:phase]:
                continue
            rows.append(index if name == order[phase] else slice(None))
        return ref.at[tuple(rows) + (slice(c0, c1),)]

    def y_copies(p, phase):
        c0, c1, order = PARTS[p]
        axis = order[phase]
        made = []
        for d in range(1, 4):
            mine = {"y": (y + d) % 4, "z": (z + d) % 4, "x": (x + d) % 4}[axis]
            src = y_pick((ysend, y2send, y3send)[phase], order, phase, mine, c0, c1)
            lead = (slice(None),) * (2 - phase)
            dst = (y1, y2, y3)[phase].at[(d - 1,) + lead + (slice(c0, c1),)]
            dev = at(d * (axis == "y"), d * (axis == "z"), d * (axis == "x"))
            made.append(remote(src, dst, y_ssem.at[phase * 3 + p], y_rsem.at[phase * 3 + p], dev))
        return made

    def y_region(p, phase):
        c0, c1, _ = PARTS[p]
        lead = (slice(None),) * (3 - phase)
        return (y1, y2, y3)[phase].at[lead + (slice(c0, c1),)]

    def y_total(p, phase):
        c0, c1, order = PARTS[p]
        await_bytes(y_region(p, phase), y_rsem.at[phase * 3 + p])
        mine = {"y": y, "z": z, "x": x}[order[phase]]
        total = y_pick((ysend, y2send, y3send)[phase], order, phase, mine, c0, c1)[...].astype(F32)
        lead = (slice(None),) * (2 - phase)
        for d in range(3):
            total = total + (y1, y2, y3)[phase][(d,) + lead + (slice(c0, c1),)].astype(F32)
        return total

    for p, (c0, c1, _) in enumerate(PARTS):
        for c in range(c0 * 2, c1 * 2):
            part = dot_nn(attended, wv[:, c * 512 : (c + 1) * 512])
            for j in range(4):
                ystg[pl.ds(c * 4 + j, N, stride=64), :] = part[:, j * HD : (j + 1) * HD]

        def pack(i, _, c0=c0, c1=c1):
            rows = ystg[pl.ds(pl.multiple_of(i * 64 + c0 * 8, 8), (c1 - c0) * 8), :]
            ysend[i // 16, i // 4 % 4, i % 4, c0:c1] = rows.astype(BF16).reshape(c1 - c0, 8, HD)
            return 0

        lax.fori_loop(0, N, pack, 0, unroll=4)
        for copy in y_copies(p, 0):
            copy.start()
    for p, (c0, c1, _) in enumerate(PARTS):
        y2send[:, :, c0:c1] = y_total(p, 0).astype(BF16)
        for copy in y_copies(p, 1):
            copy.start()
    for p, (c0, c1, _) in enumerate(PARTS):
        y3send[:, c0:c1] = y_total(p, 1)
        for copy in y_copies(p, 2):
            copy.start()
    for p, (c0, c1, _) in enumerate(PARTS):
        out_ref[c0 * 8 : c1 * 8, :] = y_total(p, 2).reshape((c1 - c0) * 8, HD)

    for phase in range(3):
        for p in range(3):
            await_bytes(q_region(phase, p), q_ssem.at[phase * 3 + p])
            await_bytes(y_region(p, phase), y_ssem.at[phase * 3 + p])
        await_bytes((rx, rz, ry)[phase].at[0:3], p_ssem.at[phase])
        await_bytes((p2x, p2z, p2y)[phase].at[0:3], p_ssem.at[3 + phase])
    for r in range(REQS):
        await_bytes(orecv.at[0:63, r], o_ssem.at[r])
    await_bytes(srecv.at[0:63], s_ssem)
    for copy in keep_copies:
        copy.wait()


def local(
    queries, new_kv, prefix_kv, pool, out_weight, parents, tail_table, fresh_slots, tail_lengths
):
    def rows_of(a):
        lead = a.shape[:-2]
        a = a.reshape(lead + (2, KVH, HD))
        k = len(lead)
        return a.transpose(tuple(range(k)) + (k + 1, k, k + 2))

    kv = rows_of(prefix_kv).reshape(REQS, PRE * TOKROWS, HD)
    pool_rows = rows_of(pool).reshape(BLK, 2, 4, 4, 8, HD)
    new_rows = rows_of(new_kv).reshape(TOKROWS, HD)
    smem = pl.BlockSpec(memory_space=pltpu.SMEM)
    vmem = pl.BlockSpec(memory_space=pltpu.VMEM)
    hbm = pl.BlockSpec(memory_space=pl.ANY)
    dma = pltpu.SemaphoreType.DMA
    out, new_pool = pl.pallas_call(
        kernel,
        out_shape=(
            jax.ShapeDtypeStruct((64, HD), F32),
            jax.ShapeDtypeStruct((BLK, 2, 4, 4, 8, HD), BF16),
        ),
        in_specs=[smem] * 4 + [vmem, vmem, hbm, hbm, hbm],
        out_specs=(vmem, hbm),
        scratch_shapes=[
            pltpu.VMEM((CHUNKS, CHUNK * TOKROWS, HD), BF16),
            pltpu.VMEM((CHUNK * TOKROWS, HD), F32),
            pltpu.VMEM((REQS, KVH, 2, PRE, HD), BF16),
            pltpu.VMEM((KVH, 2, CHUNK, HD), BF16),
            pltpu.VMEM((2, 3, 2, 4, 4, 8, HD), BF16),
            pltpu.VMEM((2, 2, 4, 4, 8, HD), BF16),
            pltpu.VMEM((BEAMS * HQ, HD), F32),
            pltpu.VMEM((4, 4, 4, KVH, GROUPS, HD), BF16),
            pltpu.VMEM((REQS, KVH, 128, HD), BF16),
            pltpu.VMEM((N, 128), F32),
            pltpu.VMEM((REQS, HQ, BEAMS, HD), BF16),
            pltpu.VMEM((N, REQS, BEAMS, HD), BF16),
            pltpu.VMEM((HQ, 128), F32),
            pltpu.VMEM((128, 128), F32),
            pltpu.VMEM((HD, 8192), BF16),
            pltpu.VMEM((N * 64, HD), F32),
            pltpu.VMEM((4, 4, 4, 8, 8, HD), BF16),
            pltpu.VMEM((3, 4, 4, 8, 8, HD), BF16),
            pltpu.VMEM((4, 4, 8, 8, HD), BF16),
            pltpu.VMEM((3, 4, 8, 8, HD), BF16),
            pltpu.VMEM((4, 8, 8, HD), F32),
            pltpu.VMEM((3, 8, 8, HD), F32),
            pltpu.VMEM((4, 2, 3, 2, 4, 8, HD), BF16),
            pltpu.VMEM((4, 4, 2, 3, 2, 8, HD), BF16),
            pltpu.VMEM((4, 4, 4, 3, 8, HD), BF16),
            pltpu.VMEM((4, 4, 4, 8, HD), BF16),
            pltpu.VMEM((4, 4, 4, 8, HD), BF16),
            pltpu.VMEM((4, 4, 4, 8, HD), BF16),
            pltpu.VMEM((4, 4, 4, 8, HD), BF16),
            pltpu.VMEM((2, 2, 4, 4, 8, HD), BF16),
            dma((CHUNKS,)), dma((4,)), dma((3,)),
            dma((9,)), dma((9,)), dma((REQS,)), dma((REQS,)), dma, dma,
            dma((9,)), dma((9,)), dma((6,)), dma((6,)),
        ],
        compiler_params=pltpu.CompilerParams(
            collective_id=0, has_side_effects=True, vmem_limit_bytes=56 << 20
        ),
        name="beam_decode",
    )(
        parents, tail_table.T, fresh_slots, tail_lengths,
        queries, new_rows, kv, pool_rows, out_weight,
    )
    new_pool = new_pool.reshape(BLK, 16, KVH, 2, HD).transpose(0, 1, 3, 2, 4)
    return out.reshape(1, 8192), new_pool.reshape(BLK, 16, 2, KVH * HD)


def solution(mesh):
    in_specs = (
        P(("req", "ctx"), None),
        P(("req", "ctx"), None, None),
        P("req", "ctx", None, None),
        P(("req", "ctx"), None, None, None),
        P("ctx", None),
        P("req"),
        P("req", None),
        P("req"),
        P("req"),
    )
    out_specs = (P(("req", "ctx"), None), P(("req", "ctx"), None, None, None))
    return jax.shard_map(local, mesh=mesh, in_specs=in_specs, out_specs=out_specs, check_vma=False)
```

time: 88.9 us -> 84.2 us (0.947)
  Pallas kernels: 84.4 us -> 79.7 us
    pallas_call x1, Pallas kernels: 84.4 us -> 79.7 us  [local(): pl.pallas_call(kernel, out_shape=(jax.ShapeDtypeStruct((64, HD), F32), ja...]
where the time goes in v2:
time: 84.2 us; the launch traced here: 84 us
  Pallas kernels  79.7 us (95%)
  local copies, waits for them, and re-layouts  3.57 us (4%)
    pallas_call x1, Pallas kernels, local(): pl.pallas_call(kernel, out_shape=(jax.ShapeDtypeStruct((64, HD), F32), ja...  79.7 us
    unnamed x2, local copies, waits for them, and re-layouts  3.57 us

profile of v2, /device:TPU:0, one launch (start us, length us, event | category | flops | bytes accessed | tf_op | source)
XLA Modules:
  0.0 84.0 jit_solution(14834651416938472940)
XLA Ops:
  0.6 79.7 %beam_decode.1 = (f32[64,128]{1,0:T(8,128)}, bf16[8,2,4,4,8,128]{5,4,3,2,1,0:T(8,128)(2,1)}) custom-call(s32[64]{0:T(128)} %parents.1, s32[4,64]{1,0:T(4,128)} %bitcast.27, s32[64]{0:T(128)} %fresh.1, s32[64]{0:T(128)} %lens.1, bf16[1,8192]{1,0:T(2,128)(2,1)} %q_ref.1, bf16[16,128]{1,0:T(8,128)(2,1)} %bitcast.26, bf16[4,16384,128]{2,1,0:T(8,128)(2,1)} %bitcast.22, ...), custom_call_target="tpu_custom_call" | custom-call | tf_op jit(solution)/shard_map/beam_decode/pallas_call | solution.py:449
  80.4 1.4 %copy.17 = f32[1,8192]{1,0:T(1,128)} copy(f32[1,8192]{1,0:T(1,128)} %bitcast.25) | data formatting | bytes 65536
  81.8 2.2 %copy.18 = bf16[8,16,2,1024]{3,2,1,0:T(2,128)(2,1)} copy(bf16[8,16,2,1024]{3,2,1,0:T(2,128)(2,1)} %bitcast.24) | data formatting | bytes 1048576

commit v3 on v2

--- a/solution.py
+++ b/solution.py
@@ -42,7 +42,7 @@
     parents, table, fresh, lens, q_ref, newkv_ref, kv_hbm, pool_hbm, w_hbm,
     out_ref, newpool_ref,
     raw, stg, kd, kt, poolv, poolz, qstg, qbuf, qd, bias, osend, orecv, stat, srecv,
-    wv, ystg, ysend, y1, y2send, y2, y3send, y3, rx, rz, ry, p2send, p2x, p2z, p2y, blk,
+    wv, ystg, ysend, yrecv, rx, rz, ry, p2send, p2x, p2z, p2y, blk,
     kv_sem, misc_sem, out_sem, q_ssem, q_rsem, o_ssem, o_rsem, s_ssem, s_rsem,
     y_ssem, y_rsem, p_ssem, p_rsem,
 ):
@@ -52,6 +52,9 @@
 
     def at(dy, dz, dx):
         return ((y + dy) % 4 * 4 + (z + dz) % 4) * 4 + (x + dx) % 4
+
+    def peer(k):
+        return at(k // 16, k // 4 % 4, k % 4)
 
     def remote(src, dst, ssem, rsem, dev):
         return pltpu.make_async_remote_copy(
@@ -81,8 +84,12 @@
     w_copy = pltpu.make_async_copy(w_hbm, wv, misc_sem.at[3])
     for copy in pool_copies:
         copy.start()
-    for c in range(CHUNKS):
+
+    def start_kv(c, _):
         kv_copy(c).start()
+        return 0
+
+    lax.fori_loop(0, CHUNKS, start_kv, 0)
     w_copy.start()
 
     for h in range(HQ):
@@ -127,6 +134,12 @@
 
     for copy in pool_copies:
         copy.wait()
+    keep_copies = [
+        pltpu.make_async_copy(poolv.at[0], newpool_ref.at[0:3], out_sem.at[0]),
+        pltpu.make_async_copy(poolv.at[1], newpool_ref.at[3:6], out_sem.at[1]),
+    ]
+    for copy in keep_copies:
+        copy.start()
 
     def spread(dst, base):
         for j in range(TOKROWS):
@@ -196,7 +209,7 @@
         bias[pl.ds(i, 1), :] = jnp.where(live, 0.0, NEG)
         return 0
 
-    lax.fori_loop(0, N, mask_row, 0, unroll=8)
+    lax.fori_loop(0, N, mask_row, 0, unroll=2)
 
     def chunks(lo, hi):
         def body(c, _):
@@ -247,9 +260,7 @@
     def group_of(t):
         return (own_group + t) % KVH
 
-    def attend(t):
-        r = t // KVH
-        g = group_of(t)
+    def attend(r, g):
         bias_r = bias[pl.ds(pl.multiple_of(r * BEAMS, BEAMS), BEAMS), :]
         bias_q = jnp.broadcast_to(bias_r[None], (GROUPS, BEAMS, 128)).reshape(128, 128)
         m_spot = lane16 == sub16 + r * BEAMS
@@ -269,48 +280,90 @@
         rows = pl.ds(pl.multiple_of(g * GROUPS, GROUPS), GROUPS)
         stat[rows, :] = stat[rows, :] + both.sum(1)
 
-    def send(t, last):
-        r = t // KVH
-        g = group_of(t)
-        for j in range(GROUPS):
+    def send(half, g):
+        pair = pl.ds(half * 2, 2)
+
+        def to(j, _):
             dev = g * GROUPS + (me + j) % GROUPS
-
-            def start(dev=dev):
-                remote(osend.at[r, dev], orecv.at[me, r], o_ssem.at[r], o_rsem.at[r], dev).start()
-                if last:
-                    remote(
-                        stat.at[pl.ds(dev, 1)], srecv.at[pl.ds(me, 1)], s_ssem, s_rsem, dev
-                    ).start()
-
-            if j == 0:
-                pl.when(t % KVH != 0)(start)
-            else:
-                start()
-
-    def steps(lo, hi, last):
-        def step(t, _):
-            send(t - 1, last)
-            attend(t)
+            remote(
+                osend.at[pair, dev], orecv.at[me, pair], o_ssem.at[half], o_rsem.at[half], dev
+            ).start()
+
+            @pl.when(half == 1)
+            def _():
+                remote(stat.at[pl.ds(dev, 1)], srecv.at[pl.ds(me, 1)], s_ssem, s_rsem, dev).start()
+
             return 0
 
-        lax.fori_loop(lo, hi, step, 0)
-
-    attend(0)
-    steps(1, 8, False)
-    leg1_wait(2)
-    lax.fori_loop(0, N, pick, 0, unroll=8)
-    leg2(0)
-    steps(8, 16, False)
-    leg2_wait(0)
-    leg2(1)
-    steps(16, 25, False)
+        lax.fori_loop(jnp.where(g == own_group, 1, 0), GROUPS, to, 0)
+
+    def step(u, _):
+        @pl.when(u == 6)
+        def _():
+            leg1_wait(2)
+            lax.fori_loop(0, N, pick, 0, unroll=8)
+            leg2(0)
+
+        @pl.when(u == 11)
+        def _():
+            leg2_wait(0)
+            leg2(1)
+
+        half = u // KVH
+        g = group_of(u)
+        attend(half * 2, g)
+        attend(half * 2 + 1, g)
+        send(half, g)
+        return 0
+
+    lax.fori_loop(0, 2 * KVH, step, 0)
     leg2_wait(1)
     leg2(2)
-    steps(25, 32, True)
-    send(jnp.int32(31), True)
-    for r in range(REQS):
-        orecv[me, r] = osend[r, me]
+    orecv[me] = osend[:, me]
     srecv[pl.ds(me, 1), :] = stat[pl.ds(me, 1), :]
+
+    await_bytes(srecv.at[0:63], s_rsem)
+    turned = srecv[...].T
+    valid = lax.broadcasted_iota(jnp.int32, (64, 128), 1) < N
+    tops = jnp.where(valid, turned[0:64], -3e38)
+    sums = jnp.where(valid, turned[64:128], 0.0)
+    top = tops.max(-1, keepdims=True)
+    share = jnp.exp2((tops - top) * SCALE)
+    share = share / (share * sums).sum(-1, keepdims=True)
+    for half in range(2):
+        await_bytes(orecv.at[0:63, half * 2 : half * 2 + 2], o_rsem.at[half])
+
+    def merge(s, carry):
+        acc, turning = carry
+        for k in range(4):
+            acc = acc + turning[:, k : k + 1] * orecv[s * 4 + k].reshape(64, HD).astype(F32)
+        return acc, pltpu.roll(turning, 124, 1)
+
+    acc, _ = lax.fori_loop(0, N // 4, merge, (jnp.zeros((64, HD), F32), share))
+    attended = acc.astype(BF16)
+
+    w_copy.wait()
+
+    def project(c, _):
+        part = dot_nn(attended, wv[:, pl.ds(pl.multiple_of(c * 512, 512), 512)])
+        for j in range(4):
+            ystg[pl.ds(c * 4 + j, N, stride=72), :] = part[:, j * HD : (j + 1) * HD]
+        return 0
+
+    lax.fori_loop(0, 16, project, 0)
+
+    def pack(i):
+        ysend[i] = ystg[pl.ds(pl.multiple_of(i * 72, 8), 64), :].astype(BF16)
+
+    def send_y(k, _):
+        j = peer(k)
+        pack(j)
+        remote(ysend.at[j], yrecv.at[me], y_ssem, y_rsem, j).start()
+        return 0
+
+    lax.fori_loop(1, N, send_y, 0)
+    own = ystg[pl.ds(pl.multiple_of(me * 72, 8), 64), :]
+    yrecv[me] = jnp.zeros((64, HD), BF16)
 
     leg2_wait(2)
     par = parents[me]
@@ -331,101 +384,28 @@
             at_t = (b, t // 8, t // 2 % 4, slice(t % 2 * 2, t % 2 * 2 + 2))
             old = poolz[at_t].astype(F32).reshape(TOKROWS, HD)
             blk[at_t] = jnp.where(here, token, old).astype(BF16).reshape(2, 8, HD)
-    keep_copies = [
-        pltpu.make_async_copy(poolv.at[0], newpool_ref.at[0:3], out_sem.at[0]),
-        pltpu.make_async_copy(poolv.at[1], newpool_ref.at[3:6], out_sem.at[1]),
-        pltpu.make_async_copy(blk, newpool_ref.at[6:8], out_sem.at[2]),
-    ]
-    for copy in keep_copies:
-        copy.start()
-
-    await_bytes(srecv.at[0:63], s_rsem)
-    turned = srecv[...].T
-    valid = lax.broadcasted_iota(jnp.int32, (64, 128), 1) < N
-    tops = jnp.where(valid, turned[0:64], -3e38)
-    sums = jnp.where(valid, turned[64:128], 0.0)
-    top = tops.max(-1, keepdims=True)
-    share = jnp.exp2((tops - top) * SCALE)
-    share = share / (share * sums).sum(-1, keepdims=True)
-    for r in range(REQS):
-        await_bytes(orecv.at[0:63, r], o_rsem.at[r])
-    acc = jnp.zeros((64, HD), F32)
-    for s in range(N):
-        acc = acc + share[:, s : s + 1] * orecv[s].reshape(64, HD).astype(F32)
-    attended = acc.astype(BF16)
-
-    w_copy.wait()
-
-    def y_pick(ref, order, phase, index, c0, c1):
-        rows = []
-        for name in "yzx":
-            if name in order[:phase]:
-                continue
-            rows.append(index if name == order[phase] else slice(None))
-        return ref.at[tuple(rows) + (slice(c0, c1),)]
-
-    def y_copies(p, phase):
-        c0, c1, order = PARTS[p]
-        axis = order[phase]
-        made = []
-        for d in range(1, 4):
-            mine = {"y": (y + d) % 4, "z": (z + d) % 4, "x": (x + d) % 4}[axis]
-            src = y_pick((ysend, y2send, y3send)[phase], order, phase, mine, c0, c1)
-            lead = (slice(None),) * (2 - phase)
-            dst = (y1, y2, y3)[phase].at[(d - 1,) + lead + (slice(c0, c1),)]
-            dev = at(d * (axis == "y"), d * (axis == "z"), d * (axis == "x"))
-            made.append(remote(src, dst, y_ssem.at[phase * 3 + p], y_rsem.at[phase * 3 + p], dev))
-        return made
-
-    def y_region(p, phase):
-        c0, c1, _ = PARTS[p]
-        lead = (slice(None),) * (3 - phase)
-        return (y1, y2, y3)[phase].at[lead + (slice(c0, c1),)]
-
-    def y_total(p, phase):
-        c0, c1, order = PARTS[p]
-        await_bytes(y_region(p, phase), y_rsem.at[phase * 3 + p])
-        mine = {"y": y, "z": z, "x": x}[order[phase]]
-        total = y_pick((ysend, y2send, y3send)[phase], order, phase, mine, c0, c1)[...].astype(F32)
-        lead = (slice(None),) * (2 - phase)
-        for d in range(3):
-            total = total + (y1, y2, y3)[phase][(d,) + lead + (slice(c0, c1),)].astype(F32)
+    new_copy = pltpu.make_async_copy(blk, newpool_ref.at[6:8], out_sem.at[2])
+    new_copy.start()
+
+    await_bytes(yrecv.at[0:63], y_rsem)
+
+    def add(s, total):
+        for k in range(4):
+            total = total + yrecv[s * 4 + k].astype(F32)
         return total
 
-    for p, (c0, c1, _) in enumerate(PARTS):
-        for c in range(c0 * 2, c1 * 2):
-            part = dot_nn(attended, wv[:, c * 512 : (c + 1) * 512])
-            for j in range(4):
-                ystg[pl.ds(c * 4 + j, N, stride=64), :] = part[:, j * HD : (j + 1) * HD]
-
-        def pack(i, _, c0=c0, c1=c1):
-            rows = ystg[pl.ds(pl.multiple_of(i * 64 + c0 * 8, 8), (c1 - c0) * 8), :]
-            ysend[i // 16, i // 4 % 4, i % 4, c0:c1] = rows.astype(BF16).reshape(c1 - c0, 8, HD)
-            return 0
-
-        lax.fori_loop(0, N, pack, 0, unroll=4)
-        for copy in y_copies(p, 0):
-            copy.start()
-    for p, (c0, c1, _) in enumerate(PARTS):
-        y2send[:, :, c0:c1] = y_total(p, 0).astype(BF16)
-        for copy in y_copies(p, 1):
-            copy.start()
-    for p, (c0, c1, _) in enumerate(PARTS):
-        y3send[:, c0:c1] = y_total(p, 1)
-        for copy in y_copies(p, 2):
-            copy.start()
-    for p, (c0, c1, _) in enumerate(PARTS):
-        out_ref[c0 * 8 : c1 * 8, :] = y_total(p, 2).reshape((c1 - c0) * 8, HD)
+    out_ref[...] = lax.fori_loop(0, N // 4, add, own)
 
     for phase in range(3):
         for p in range(3):
             await_bytes(q_region(phase, p), q_ssem.at[phase * 3 + p])
-            await_bytes(y_region(p, phase), y_ssem.at[phase * 3 + p])
         await_bytes((rx, rz, ry)[phase].at[0:3], p_ssem.at[phase])
         await_bytes((p2x, p2z, p2y)[phase].at[0:3], p_ssem.at[3 + phase])
-    for r in range(REQS):
-        await_bytes(orecv.at[0:63, r], o_ssem.at[r])
+    for half in range(2):
+        await_bytes(orecv.at[0:63, half * 2 : half * 2 + 2], o_ssem.at[half])
     await_bytes(srecv.at[0:63], s_ssem)
+    await_bytes(ysend.at[0:63], y_ssem)
+    new_copy.wait()
     for copy in keep_copies:
         copy.wait()
 
@@ -470,13 +450,9 @@
             pltpu.VMEM((HQ, 128), F32),
             pltpu.VMEM((128, 128), F32),
             pltpu.VMEM((HD, 8192), BF16),
-            pltpu.VMEM((N * 64, HD), F32),
-            pltpu.VMEM((4, 4, 4, 8, 8, HD), BF16),
-            pltpu.VMEM((3, 4, 4, 8, 8, HD), BF16),
-            pltpu.VMEM((4, 4, 8, 8, HD), BF16),
-            pltpu.VMEM((3, 4, 8, 8, HD), BF16),
-            pltpu.VMEM((4, 8, 8, HD), F32),
-            pltpu.VMEM((3, 8, 8, HD), F32),
+            pltpu.VMEM((N * 72, HD), F32),
+            pltpu.VMEM((N, 64, HD), BF16),
+            pltpu.VMEM((N, 64, HD), BF16),
             pltpu.VMEM((4, 2, 3, 2, 4, 8, HD), BF16),
             pltpu.VMEM((4, 4, 2, 3, 2, 8, HD), BF16),
             pltpu.VMEM((4, 4, 4, 3, 8, HD), BF16),
@@ -486,8 +462,8 @@
             pltpu.VMEM((4, 4, 4, 8, HD), BF16),
             pltpu.VMEM((2, 2, 4, 4, 8, HD), BF16),
             dma((CHUNKS,)), dma((4,)), dma((3,)),
-            dma((9,)), dma((9,)), dma((REQS,)), dma((REQS,)), dma, dma,
-            dma((9,)), dma((9,)), dma((6,)), dma((6,)),
+            dma((9,)), dma((9,)), dma((2,)), dma((2,)), dma, dma,
+            dma, dma, dma((6,)), dma((6,)),
         ],
         compiler_params=pltpu.CompilerParams(
             collective_id=0, has_side_effects=True, vmem_limit_bytes=56 << 20

time: 84.2 us -> 80.1 us (0.951)
  Pallas kernels: 79.7 us -> 75.6 us
    pallas_call x1, Pallas kernels: 79.7 us -> 75.6 us  [local(): pl.pallas_call(kernel, out_shape=(jax.ShapeDtypeStruct((64, HD), F32), ja...]
where the time goes in v3:
time: 80.1 us; the launch traced here: 79.8 us
  Pallas kernels  75.6 us (94%)
  local copies, waits for them, and re-layouts  3.57 us (4%)
    pallas_call x1, Pallas kernels, local(): pl.pallas_call(kernel, out_shape=(jax.ShapeDtypeStruct((64, HD), F32), ja...  75.6 us
    unnamed x2, local copies, waits for them, and re-layouts  3.57 us

profile of v3, /device:TPU:0, one launch (start us, length us, event | category | flops | bytes accessed | tf_op | source)
XLA Modules:
  0.0 79.8 jit_solution(10488831328477361677)
XLA Ops:
  0.6 75.6 %beam_decode.1 = (f32[64,128]{1,0:T(8,128)}, bf16[8,2,4,4,8,128]{5,4,3,2,1,0:T(8,128)(2,1)}) custom-call(s32[64]{0:T(128)} %parents.1, s32[4,64]{1,0:T(4,128)} %bitcast.27, s32[64]{0:T(128)} %fresh.1, s32[64]{0:T(128)} %lens.1, bf16[1,8192]{1,0:T(2,128)(2,1)} %q_ref.1, bf16[16,128]{1,0:T(8,128)(2,1)} %bitcast.26, bf16[4,16384,128]{2,1,0:T(8,128)(2,1)} %bitcast.22, ...), custom_call_target="tpu_custom_call" | custom-call | tf_op jit(solution)/shard_map/beam_decode/pallas_call | solution.py:429
  76.3 1.4 %copy.17 = f32[1,8192]{1,0:T(1,128)} copy(f32[1,8192]{1,0:T(1,128)} %bitcast.25) | data formatting | bytes 65536
  77.6 2.2 %copy.18 = bf16[8,16,2,1024]{3,2,1,0:T(2,128)(2,1)} copy(bf16[8,16,2,1024]{3,2,1,0:T(2,128)(2,1)} %bitcast.24) | data formatting | bytes 1048576

commit v4 on v3

--- a/solution.py
+++ b/solution.py
@@ -193,6 +193,16 @@
     def leg2_wait(phase):
         await_bytes((p2x, p2z, p2y)[phase].at[0:3], p_rsem.at[3 + phase])
 
+    def chunks(lo, hi):
+        def body(c, _):
+            kv_copy(c).wait()
+            stg[...] = raw[c].astype(F32)
+            spread(kd.at[c // PER_REQ], pl.multiple_of(c % PER_REQ * CHUNK, CHUNK))
+            return 0
+
+        lax.fori_loop(lo, hi, body, 0)
+
+    chunks(0, 4)
     pl.semaphore_wait(barrier, 9)
     q_send(0)
     leg1(0)
@@ -209,25 +219,17 @@
         bias[pl.ds(i, 1), :] = jnp.where(live, 0.0, NEG)
         return 0
 
-    lax.fori_loop(0, N, mask_row, 0, unroll=2)
-
-    def chunks(lo, hi):
-        def body(c, _):
-            kv_copy(c).wait()
-            stg[...] = raw[c].astype(F32)
-            spread(kd.at[c // PER_REQ], pl.multiple_of(c % PER_REQ * CHUNK, CHUNK))
-            return 0
-
-        lax.fori_loop(lo, hi, body, 0)
-
+    lax.fori_loop(0, N, mask_row, 0, unroll=8)
+
+    chunks(4, 10)
     q_wait(0)
     q_send(1)
-    chunks(0, 8)
+    chunks(10, 20)
     q_wait(1)
     q_send(2)
     leg1_wait(0)
     leg1(1)
-    chunks(8, 32)
+    chunks(20, 32)
     q_wait(2)
     leg1_wait(1)
     leg1(2)
@@ -247,10 +249,11 @@
     lane16 = lax.broadcasted_iota(jnp.int32, (BEAMS, 128), 1)
 
     def turn(r, _):
-        qstg[...] = qbuf[r].reshape(BEAMS * HQ, HD).astype(F32)
+        for i in range(BEAMS):
+            qstg[i * 72 : i * 72 + HQ, :] = qbuf[r, i // 4, i % 4].reshape(HQ, HD).astype(F32)
         for h in range(HQ):
             qd[r, h // GROUPS, h % GROUPS * BEAMS : (h % GROUPS + 1) * BEAMS, :] = qstg[
-                pl.ds(h, BEAMS, stride=HQ), :
+                pl.ds(h, BEAMS, stride=72), :
             ].astype(BF16)
         return 0
 
@@ -350,7 +353,7 @@
             ystg[pl.ds(c * 4 + j, N, stride=72), :] = part[:, j * HD : (j + 1) * HD]
         return 0
 
-    lax.fori_loop(0, 16, project, 0)
+    lax.fori_loop(0, 16, project, 0, unroll=4)
 
     def pack(i):
         ysend[i] = ystg[pl.ds(pl.multiple_of(i * 72, 8), 64), :].astype(BF16)
@@ -361,7 +364,7 @@
         remote(ysend.at[j], yrecv.at[me], y_ssem, y_rsem, j).start()
         return 0
 
-    lax.fori_loop(1, N, send_y, 0)
+    lax.fori_loop(1, N, send_y, 0, unroll=3)
     own = ystg[pl.ds(pl.multiple_of(me * 72, 8), 64), :]
     yrecv[me] = jnp.zeros((64, HD), BF16)
 
@@ -441,7 +444,7 @@
             pltpu.VMEM((KVH, 2, CHUNK, HD), BF16),
             pltpu.VMEM((2, 3, 2, 4, 4, 8, HD), BF16),
             pltpu.VMEM((2, 2, 4, 4, 8, HD), BF16),
-            pltpu.VMEM((BEAMS * HQ, HD), F32),
+            pltpu.VMEM((BEAMS * 72, HD), F32),
             pltpu.VMEM((4, 4, 4, KVH, GROUPS, HD), BF16),
             pltpu.VMEM((REQS, KVH, 128, HD), BF16),
             pltpu.VMEM((N, 128), F32),

time: 80.1 us -> 75.6 us (0.944)
  Pallas kernels: 75.6 us -> 71.1 us
    pallas_call x1, Pallas kernels: 75.6 us -> 71.1 us  [local(): pl.pallas_call(kernel, out_shape=(jax.ShapeDtypeStruct((64, HD), F32), ja...]
where the time goes in v4:
time: 75.6 us; the launch traced here: 75.4 us
  Pallas kernels  71.1 us (94%)
  local copies, waits for them, and re-layouts  3.57 us (5%)
    pallas_call x1, Pallas kernels, local(): pl.pallas_call(kernel, out_shape=(jax.ShapeDtypeStruct((64, HD), F32), ja...  71.1 us
    unnamed x2, local copies, waits for them, and re-layouts  3.57 us

profile of v4, /device:TPU:0, one launch (start us, length us, event | category | flops | bytes accessed | tf_op | source)
XLA Modules:
  0.0 75.4 jit_solution(6974784261937454663)
XLA Ops:
  0.6 71.1 %beam_decode.1 = (f32[64,128]{1,0:T(8,128)}, bf16[8,2,4,4,8,128]{5,4,3,2,1,0:T(8,128)(2,1)}) custom-call(s32[64]{0:T(128)} %parents.1, s32[4,64]{1,0:T(4,128)} %bitcast.27, s32[64]{0:T(128)} %fresh.1, s32[64]{0:T(128)} %lens.1, bf16[1,8192]{1,0:T(2,128)(2,1)} %q_ref.1, bf16[16,128]{1,0:T(8,128)(2,1)} %bitcast.26, bf16[4,16384,128]{2,1,0:T(8,128)(2,1)} %bitcast.22, ...), custom_call_target="tpu_custom_call" | custom-call | tf_op jit(solution)/shard_map/beam_decode/pallas_call | solution.py:432
  71.8 1.4 %copy.17 = f32[1,8192]{1,0:T(1,128)} copy(f32[1,8192]{1,0:T(1,128)} %bitcast.25) | data formatting | bytes 65536
  73.2 2.2 %copy.18 = bf16[8,16,2,1024]{3,2,1,0:T(2,128)(2,1)} copy(bf16[8,16,2,1024]{3,2,1,0:T(2,128)(2,1)} %bitcast.24) | data formatting | bytes 1048576
